TPU v7x, 32 devices: a whole 2x2x4 slice. The times are simulated.
32 devices in a mesh: blk: 16 (over z, y, x), col: 2 (over core).
Axes of the slice: x: 2, y: 2, z: 4, core: 2. Of those that a mesh axis runs over, the one named last changes fastest.
Arguments:
- queries: bfloat16 [128, 16384], P('blk', 'col'), may hold values from -6 to 6
- factor: bfloat16 [16384, 1024], P('col', 'blk'), may hold values from -0.046875 to 0.046875
- eigenvalues: float32 [1024], replicated, may hold values from 0.05 to 20
- damping: float32 [1], replicated, may hold values from 0.5 to 2
- train_rows: bfloat16 [16384, 16384], P('blk', 'col'), may hold values from -0.046875 to 0.046875
Outputs:
- scores: bfloat16 [128, 16384], P('col', 'blk')
All inputs are finite; a program needn't handle non-finite values.
Results may differ from a plain program's by a relative error of at most 0.0049.
Values may be sent and summed in bfloat16 or wider, within the bound.
A program may use at most 64 MiB of HBM per device.

v0:
```python
import jax
import jax.numpy as jnp
from jax import lax
from jax.sharding import PartitionSpec as P


def per_device(queries, factor, eigenvalues, damping, train_rows):
    damp_value = damping[0]
    weights = eigenvalues / (eigenvalues + damp_value)
    query_part = lax.all_to_all(queries, "blk", split_axis=1, concat_axis=0, tiled=True)
    factor_part = lax.all_to_all(factor, "blk", split_axis=0, concat_axis=1, tiled=True)
    partial_value = jnp.dot(query_part, factor_part, preferred_element_type=jnp.float32)
    coefficient = lax.psum(partial_value, ("blk", "col"))
    scaled = coefficient * weights[None, :]
    correction = jnp.dot(scaled, factor_part.astype(jnp.float32).T, precision=lax.Precision.HIGHEST)
    pre_part = ((query_part.astype(jnp.float32) - correction) / damp_value).astype(jnp.bfloat16)
    pre_all = lax.all_gather(pre_part, "blk", axis=1, tiled=True)
    partial_scores = jnp.einsum(
        "qk,nk->qn", pre_all, train_rows, preferred_element_type=jnp.float32
    )
    scores = lax.psum_scatter(partial_scores, "col", scatter_dimension=0, tiled=True)
    return scores.astype(jnp.bfloat16)


def solution(mesh):
    in_specs = (P("blk", "col"), P("col", "blk"), P(), P(), P("blk", "col"))
    out_specs = P("col", "blk")
    return jax.shard_map(
        per_device, mesh=mesh, in_specs=in_specs, out_specs=out_specs, check_vma=False
    )
```

profile of v0, /device:TPU:0, one launch (start us, length us, event | category | flops | bytes accessed | tf_op | source)
XLA Modules:
  0.0 269.8 jit_solution(12998497539709083565)
XLA Ops:
  6.5 8.3 %all-to-all-start = ((bf16[8,16,512]{2,0,1:T(8,128)(2,1)}), bf16[8,16,512]{2,0,1:T(8,128)(2,1)S(1)}, u32[]{:S(2)}, u32[]{:S(2)}) async-start(bf16[8,16,512]{2,0,1:T(8,128)(2,1)} %bitcast.25), calls=%async_computation | async-start | bytes 262144 | tf_op jit(solution)/shard_map/all_to_all | solution.py:10
  14.9 0.0 all-reduce.2.cloned.1.call-start
  14.9 1.3 copy.10
  16.3 6.4 %all-to-all-done = bf16[8,16,512]{2,0,1:T(8,128)(2,1)S(1)} async-done(((bf16[8,16,512]{2,0,1:T(8,128)(2,1)}), bf16[8,16,512]{2,0,1:T(8,128)(2,1)S(1)}, u32[]{:S(2)}, u32[]{:S(2)}) %all-to-all-start) | async-done | bytes 131104 | tf_op jit(solution)/shard_map/all_to_all | solution.py:10
  22.7 28.3 %all_to_all.38 = bf16[16,512,64]{1,2,0:T(8,128)(2,1)S(1)} all-to-all(bf16[16,512,64]{1,2,0:T(8,128)(2,1)S(1)} %bitcast.21), channel_id=1, replica_groups=mesh['blk'=16,'col'=2] {'blk'}, dimensions={0} | all-to-all | bytes 2097152 | tf_op jit(solution)/shard_map/all_to_all | solution.py:11
  51.0 1.3 fusion.4
  52.3 0.0 all-reduce.2.cloned.1.call-update
  52.3 0.0 all-gather.2.cloned.1.call-start
  53.0 0.7 add_divide_fusion
  53.7 126.2 %all-reduce.2.cloned.1.call-done = f32[128,1024]{1,0:T(8,128)} async-done(((f32[128,1024]{1,0:T(8,128)}), f32[128,1024]{1,0:T(8,128)}) %all-reduce.2.cloned.1.call-update) | async-done | bytes 524304 | tf_op jit(solution)/shard_map/psum | solution.py:13
  179.9 2.3 fusion.1
  182.2 0.0 all-gather.2.cloned.1.call-update
  182.2 0.0 reduce-scatter.2.cloned.1.call-start
  182.2 60.3 %all-gather.2.cloned.1.call-done = bf16[128,8192]{1,0:T(8,128)(2,1)} async-done(((bf16[128,512]{1,0:T(8,128)(2,1)}), bf16[128,8192]{1,0:T(8,128)(2,1)}) %all-gather.2.cloned.1.call-update) | async-done | bytes 2097168 | tf_op jit(solution)/shard_map/all_gather | solution.py:17
  242.5 12.9 %fusion.6 = f32[128,1024]{1,0:T(8,128)} fusion(bf16[128,8192]{1,0:T(8,128)(2,1)} %all-gather.2.cloned.1.call-done, bf16[1024,8192]{1,0:T(8,128)(2,1)} %param.9), kind=kOutput, calls=%fused_computation.9 | convolution fusion | flops 2147483648 | bytes 19398656 | tf_op jit(solution)/shard_map/qk,nk->qn/dot_general | solution.py:18
  255.4 0.0 reduce-scatter.2.cloned.1.call-update
  255.4 6.3 %reduce-scatter.2.cloned.1.call-done = f32[64,1024]{1,0:T(8,128)} async-done(((f32[128,1024]{1,0:T(8,128)}), f32[64,1024]{1,0:T(8,128)}) %reduce-scatter.2.cloned.1.call-update) | async-done | bytes 262160 | tf_op jit(solution)/shard_map/reduce_scatter | solution.py:21
  261.7 1.6 convert_element_type.12
Async XLA Ops:
  6.5 16.1 %all-to-all-start = ((bf16[8,16,512]{2,0,1:T(8,128)(2,1)}), bf16[8,16,512]{2,0,1:T(8,128)(2,1)S(1)}, u32[]{:S(2)}, u32[]{:S(2)}) async-start(bf16[8,16,512]{2,0,1:T(8,128)(2,1)} %bitcast.25), calls=%async_computation | async-start | bytes 262144 | tf_op jit(solution)/shard_map/all_to_all | solution.py:10
  14.9 165.0 %all-reduce.2.cloned.1.call-start = ((), (), s32[]{:S(2)}) async-start(), calls=%async_computation.3 | async-start | bytes 1048576 | tf_op jit(solution)/shard_map/psum | solution.py:13
  52.3 190.2 %all-gather.2.cloned.1.call-start = ((), (), s32[]{:S(2)}) async-start(), calls=%async_computation.4 | async-start | bytes 2228224 | tf_op jit(solution)/shard_map/all_gather | solution.py:17
  182.2 79.5 %reduce-scatter.2.cloned.1.call-start = ((), (), s32[]{:S(2)}) async-start(), calls=%async_computation.5 | async-start | bytes 786432 | tf_op jit(solution)/shard_map/reduce_scatter | solution.py:21
Sparse Core Ops, SparseCore 0:
  52.4 127.3 all-reduce.1
  182.6 59.8 all-gather.1
  255.6 6.0 reduce-scatter.1
where the time goes:
time: 270 us
  waiting for transfers between devices  199 us (74%)
  blocking collectives  28.3 us (10%)
  matrix products  16.4 us (6%)
  between operations  13.8 us (5%)
  starting transfers between devices  8.47 us (3%)
    psum x1, waiting for transfers between devices, per_device(): coefficient = lax.psum(partial_value, ('blk', 'col'))  126 us
    all_gather x1, waiting for transfers between devices, per_device(): pre_all = lax.all_gather(pre_part, 'blk', axis=1, tiled=True)  60.3 us
    all_to_all x1, blocking collectives, per_device(): lax.all_to_all(factor, 'blk', split_axis=0, concat_axis=1, tiled=True)  28.3 us
    dot_general x1, matrix products, per_device(): jnp.einsum('qk,nk->qn', pre_all, train_rows, preferred_element_type=jnp.f...  12.9 us
    all_to_all x1, starting transfers between devices, per_device(): lax.all_to_all(queries, 'blk', split_axis=1, concat_axis=0, tiled=True)  8.34 us
    all_to_all x1, waiting for transfers between devices, per_device(): lax.all_to_all(queries, 'blk', split_axis=1, concat_axis=0, tiled=True)  6.41 us
    reduce_scatter x1, waiting for transfers between devices, per_device(): lax.psum_scatter(partial_scores, 'col', scatter_dimension=0, tiled=True)  6.26 us
  transfers between devices with their start and end apart: 4, of which 4 were waited for; matrix products, arithmetic and copies ran while one was open for 1% of the time, Pallas kernels for 0%

commit v1 on v0

--- a/solution.py
+++ b/solution.py
@@ -10,7 +10,7 @@
     query_part = lax.all_to_all(queries, "blk", split_axis=1, concat_axis=0, tiled=True)
     factor_part = lax.all_to_all(factor, "blk", split_axis=0, concat_axis=1, tiled=True)
     partial_value = jnp.dot(query_part, factor_part, preferred_element_type=jnp.float32)
-    coefficient = lax.psum(partial_value, ("blk", "col"))
+    coefficient = jnp.sum(lax.all_gather(partial_value, ("blk", "col")), axis=0)
     scaled = coefficient * weights[None, :]
     correction = jnp.dot(scaled, factor_part.astype(jnp.float32).T, precision=lax.Precision.HIGHEST)
     pre_part = ((query_part.astype(jnp.float32) - correction) / damp_value).astype(jnp.bfloat16)

time: 270 us -> 261 us (0.967)
  waiting for transfers between devices: 199 us -> 183 us
  other arithmetic: 2.31 us -> 9.77 us
    psum x1 -> x0, waiting for transfers between devices: 126 us -> none  [per_device(): coefficient = lax.psum(partial_value, ('blk', 'col'))]
    all_gather x0 -> x1, waiting for transfers between devices: none -> 111 us  [per_device(): coefficient = jnp.sum(lax.all_gather(partial_value, ('blk', 'col')), axis=0)]
    reduce_sum x0 -> x1, other arithmetic: none -> 7.45 us  [per_device(): coefficient = jnp.sum(lax.all_gather(partial_value, ('blk', 'col')), axis=0)]
where the time goes in v1:
time: 261 us; the launch traced here: 260 us
  waiting for transfers between devices  183 us (70%)
  blocking collectives  28.3 us (11%)
  matrix products  15.4 us (6%)
  between operations  13.8 us (5%)
  other arithmetic  9.77 us (4%)
  starting transfers between devices  8.47 us (3%)
    all_gather x1, waiting for transfers between devices, per_device(): coefficient = jnp.sum(lax.all_gather(partial_value, ('blk', 'col')), axis=0)  111 us
    all_gather x1, waiting for transfers between devices, per_device(): pre_all = lax.all_gather(pre_part, 'blk', axis=1, tiled=True)  59.2 us
    all_to_all x1, blocking collectives, per_device(): lax.all_to_all(factor, 'blk', split_axis=0, concat_axis=1, tiled=True)  28.3 us
    dot_general x1, matrix products, per_device(): jnp.einsum('qk,nk->qn', pre_all, train_rows, preferred_element_type=jnp.f...  12.9 us
    all_to_all x1, starting transfers between devices, per_device(): lax.all_to_all(queries, 'blk', split_axis=1, concat_axis=0, tiled=True)  8.34 us
    reduce_sum x1, other arithmetic, per_device(): coefficient = jnp.sum(lax.all_gather(partial_value, ('blk', 'col')), axis=0)  7.45 us
    all_to_all x1, waiting for transfers between devices, per_device(): lax.all_to_all(queries, 'blk', split_axis=1, concat_axis=0, tiled=True)  6.41 us
    reduce_scatter x1, waiting for transfers between devices, per_device(): lax.psum_scatter(partial_scores, 'col', scatter_dimension=0, tiled=True)  6.26 us
  transfers between devices with their start and end apart: 4, of which 4 were waited for; matrix products, arithmetic and copies ran while one was open for 1% of the time, Pallas kernels for 0%

profile of v1, /device:TPU:0, one launch (start us, length us, event | category | flops | bytes accessed | tf_op | source)
XLA Modules:
  0.0 260.5 jit_solution(7541901971706037716)
XLA Ops:
  6.5 8.3 %all-to-all-start = ((bf16[8,16,512]{2,0,1:T(8,128)(2,1)}), bf16[8,16,512]{2,0,1:T(8,128)(2,1)S(1)}, u32[]{:S(2)}, u32[]{:S(2)}) async-start(bf16[8,16,512]{2,0,1:T(8,128)(2,1)} %bitcast.27), calls=%async_computation | async-start | bytes 262144 | tf_op jit(solution)/shard_map/all_to_all | solution.py:10
  14.9 0.0 all-gather.6.cloned.1.call-start
  14.9 1.3 copy.10
  16.3 6.4 %all-to-all-done = bf16[8,16,512]{2,0,1:T(8,128)(2,1)S(1)} async-done(((bf16[8,16,512]{2,0,1:T(8,128)(2,1)}), bf16[8,16,512]{2,0,1:T(8,128)(2,1)S(1)}, u32[]{:S(2)}, u32[]{:S(2)}) %all-to-all-start) | async-done | bytes 131104 | tf_op jit(solution)/shard_map/all_to_all | solution.py:10
  22.7 28.3 %all_to_all.38 = bf16[16,512,64]{1,2,0:T(8,128)(2,1)S(1)} all-to-all(bf16[16,512,64]{1,2,0:T(8,128)(2,1)S(1)} %bitcast.23), channel_id=1, replica_groups=mesh['blk'=16,'col'=2] {'blk'}, dimensions={0} | all-to-all | bytes 2097152 | tf_op jit(solution)/shard_map/all_to_all | solution.py:11
  51.0 1.3 fusion.4
  52.3 0.0 all-gather.6.cloned.1.call-update
  52.3 0.0 all-gather.4.cloned.1.call-start
  53.0 0.7 add_divide_fusion
  53.7 111.5 %all-gather.6.cloned.1.call-done = f32[4096,1024]{1,0:T(8,128)} async-done(((f32[128,1024]{1,0:T(8,128)}), f32[4096,1024]{1,0:T(8,128)}) %all-gather.6.cloned.1.call-update) | async-done | bytes 16777232 | tf_op jit(solution)/shard_map/all_gather | solution.py:13
  165.2 7.5 %reduce_sum.9 = f32[128,1024]{1,0:T(8,128)S(1)} reduce(f32[32,128,1024]{2,1,0:T(8,128)} %bitcast.22, f32[]{:T(128)} %constant.0.clone.1), dimensions={0}, to_apply=%region_0.0 | reduce | flops 4063232 | bytes 17301508 | tf_op jit(solution)/shard_map/reduce_sum | solution.py:13
  172.6 1.3 fusion.1
  173.9 0.0 all-gather.4.cloned.1.call-update
  173.9 0.0 reduce-scatter.2.cloned.1.call-start
  174.0 59.2 %all-gather.4.cloned.1.call-done = bf16[128,8192]{1,0:T(8,128)(2,1)} async-done(((bf16[128,512]{1,0:T(8,128)(2,1)}), bf16[128,8192]{1,0:T(8,128)(2,1)}) %all-gather.4.cloned.1.call-update) | async-done | bytes 2097168 | tf_op jit(solution)/shard_map/all_gather | solution.py:17
  233.2 12.9 %fusion.6 = f32[128,1024]{1,0:T(8,128)} fusion(bf16[128,8192]{1,0:T(8,128)(2,1)} %all-gather.4.cloned.1.call-done, bf16[1024,8192]{1,0:T(8,128)(2,1)} %param.9), kind=kOutput, calls=%fused_computation.9 | convolution fusion | flops 2147483648 | bytes 19398656 | tf_op jit(solution)/shard_map/qk,nk->qn/dot_general | solution.py:18
  246.0 0.0 reduce-scatter.2.cloned.1.call-update
  246.1 6.3 %reduce-scatter.2.cloned.1.call-done = f32[64,1024]{1,0:T(8,128)} async-done(((f32[128,1024]{1,0:T(8,128)}), f32[64,1024]{1,0:T(8,128)}) %reduce-scatter.2.cloned.1.call-update) | async-done | bytes 262160 | tf_op jit(solution)/shard_map/reduce_scatter | solution.py:21
  252.3 1.6 convert_element_type.12
Async XLA Ops:
  6.5 16.1 %all-to-all-start = ((bf16[8,16,512]{2,0,1:T(8,128)(2,1)}), bf16[8,16,512]{2,0,1:T(8,128)(2,1)S(1)}, u32[]{:S(2)}, u32[]{:S(2)}) async-start(bf16[8,16,512]{2,0,1:T(8,128)(2,1)} %bitcast.27), calls=%async_computation | async-start | bytes 262144 | tf_op jit(solution)/shard_map/all_to_all | solution.py:10
  14.9 150.3 %all-gather.6.cloned.1.call-start = ((), (), s32[]{:S(2)}) async-start(), calls=%async_computation.5 | async-start | bytes 17301504 | tf_op jit(solution)/shard_map/all_gather | solution.py:13
  52.3 180.8 %all-gather.4.cloned.1.call-start = ((), (), s32[]{:S(2)}) async-start(), calls=%async_computation.3 | async-start | bytes 2228224 | tf_op jit(solution)/shard_map/all_gather | solution.py:17
  173.9 78.4 %reduce-scatter.2.cloned.1.call-start = ((), (), s32[]{:S(2)}) async-start(), calls=%async_computation.4 | async-start | bytes 786432 | tf_op jit(solution)/shard_map/reduce_scatter | solution.py:21
Sparse Core Ops, SparseCore 0:
  52.4 112.6 all-gather.5
  174.0 59.0 all-gather.3
  246.2 6.0 reduce-scatter.1
